TPU v7x, 32 devices: a whole 2x2x4 slice. The times are simulated.
32 devices in a mesh: mem: 16 (over z, y, core), tile: 2 (over x).
Axes of the slice: x: 2, y: 2, z: 4, core: 2. Of those that a mesh axis runs over, the one named last changes fastest.
Arguments:
- member_perturbations: float32 [3, 32, 16, 256], P(None, 'mem', None, 'tile'), may hold values from -3 to 3
- obs_index: int32 [16, 2, 256], P('mem', 'tile'), may hold values from 0 to 383
- obs_value: float32 [16, 2, 256], P('mem', 'tile'), may hold values from -4 to 4
- obs_var: float32 [16, 2, 256], P('mem', 'tile'), may hold values from 0.05 to 0.5
- loc_weight: float32 [16, 2, 256], P('mem', 'tile'), may hold values from 0.2 to 1
Outputs:
- forecast: float32 [3, 32, 16, 256], P(None, 'mem', None, 'tile')
All inputs are finite; a program needn't handle non-finite values.
Results may differ from a plain program's by a relative error of at most 0.0003.
Values sent between devices are 32-bit elements; how exact they have to be, the bound alone decides.
A program may use at most 64 MiB of HBM per device.

v0:
```python
import jax
import jax.numpy as jnp
from jax import lax
from jax.sharding import PartitionSpec as P

PCELL = 128
NSIT = 6
mean_depth = 4.0
gravity = 0.25
coriolis = 0.1
time_step = 0.3
highest = lax.Precision.HIGHEST


def with_halo(cells, sides, width):
    for axis, dim in sides:
        count = lax.axis_size(axis)
        head = lax.slice_in_dim(cells, 0, width, axis=dim)
        tail = lax.slice_in_dim(cells, cells.shape[dim] - width, cells.shape[dim], axis=dim)
        cells = jnp.concatenate(
            [
                lax.ppermute(tail, axis, [(i, (i + 1) % count) for i in range(count)]),
                cells,
                lax.ppermute(head, axis, [((i + 1) % count, i) for i in range(count)]),
            ],
            axis=dim,
        )
    return cells


def middle(field):
    return field[..., 1:-1]


def across(field):
    return (field[..., 2:] - field[..., :-2]) * 0.5


def along(field):
    inner = middle(field)
    return (jnp.roll(inner, -1, -2) - jnp.roll(inner, 1, -2)) * 0.5


def tendency(extended):
    height = extended[0]
    east_wind = extended[1]
    north_wind = extended[2]
    depth_total = mean_depth + height
    east_mid = middle(east_wind)
    north_mid = middle(north_wind)
    d_height = -(across(depth_total * east_wind) + along(depth_total * north_wind))
    d_east = (
        -(east_mid * across(east_wind) + north_mid * along(east_wind))
        - gravity * across(height)
        + coriolis * north_mid
    )
    d_north = (
        -(east_mid * across(north_wind) + north_mid * along(north_wind))
        - gravity * along(height)
        - coriolis * east_mid
    )
    return jnp.stack([d_height, d_east, d_north])


def lead_interval_number(dynamics_variables):
    extended = with_halo(dynamics_variables, (("tile", 3),), 4)
    first_slope = tendency(extended)
    slope_two = tendency(extended[..., 1:-1] + 0.5 * time_step * first_slope)
    slope_three = tendency(extended[..., 2:-2] + 0.5 * time_step * slope_two)
    slope_four = tendency(extended[..., 3:-3] + time_step * slope_three)
    dynamics_variables = dynamics_variables + time_step / 6.0 * (
        first_slope[..., 3:-3]
        + 2.0 * slope_two[..., 2:-2]
        + 2.0 * slope_three[..., 1:-1]
        + slope_four
    )
    return dynamics_variables


def product(left, right):
    return jnp.einsum("rbij,rbjk->rbik", left, right, precision=highest)


def analyse(blocks, indices, values, variances, locality):
    members = blocks.shape[1]
    row_count = blocks.shape[2]
    block_count = blocks.shape[3]
    cells = blocks.shape[4]
    xbar = jnp.mean(blocks, axis=1, keepdims=True)
    pert = blocks - xbar
    flat = jnp.transpose(blocks, (2, 3, 0, 4, 1)).reshape(
        row_count, block_count, 3 * cells, members
    )
    observed = jnp.take_along_axis(flat, indices[..., None], axis=2)
    ybar = jnp.mean(observed, axis=3, keepdims=True)
    obs_pert = observed - ybar
    weighted = obs_pert * (locality / variances)[..., None]
    gram = jnp.einsum("rboi,rboj->rbij", weighted, obs_pert, precision=highest)
    identity = jnp.eye(members, dtype=jnp.float32)
    amat = gram + (members - 1.0) * identity
    frob = jnp.sqrt(jnp.sum(amat * amat, axis=(2, 3), keepdims=True))
    ymat = amat / frob
    zmat = jnp.broadcast_to(identity, amat.shape)
    for _ in range(NSIT):
        newton = 1.5 * identity - 0.5 * product(zmat, ymat)
        ymat = product(ymat, newton)
        zmat = product(newton, zmat)
    prec = product(zmat, zmat) / frob
    wmat = jnp.sqrt((members - 1.0) / frob) * zmat
    innov = values - ybar[..., 0]
    projected = jnp.einsum("rbok,rbo->rbk", weighted, innov, precision=highest)
    wbar = jnp.einsum("rbij,rbj->rbi", prec, projected, precision=highest)
    wtot = wmat + wbar[..., None]
    return xbar + jnp.einsum("virbc,rbij->vjrbc", pert, wtot, precision=highest)


def local(member_perturbations, obs_index, obs_value, obs_var, loc_weight):
    background_member_set = lead_interval_number(member_perturbations)
    patches = lax.all_to_all(background_member_set, "mem", split_axis=2, concat_axis=1, tiled=True)
    members = patches.shape[1]
    row_count = patches.shape[2]
    columns = patches.shape[3]
    blocks = patches.reshape(3, members, row_count, columns // PCELL, PCELL)
    updated_member_set = analyse(blocks, obs_index, obs_value, obs_var, loc_weight)
    closing_solution = lax.all_to_all(
        updated_member_set.reshape(3, members, row_count, columns),
        "mem",
        split_axis=1,
        concat_axis=2,
        tiled=True,
    )
    return lead_interval_number(closing_solution)


def solution(mesh):
    in_specs = (
        P(None, "mem", None, "tile"),
        P("mem", "tile", None),
        P("mem", "tile", None),
        P("mem", "tile", None),
        P("mem", "tile", None),
    )
    out_specs = P(None, "mem", None, "tile")
    return jax.shard_map(local, mesh=mesh, in_specs=in_specs, out_specs=out_specs, check_vma=False)
```

profile of v0, /device:TPU:0, one launch (start us, length us, event | category | flops | bytes accessed | tf_op | source)
XLA Modules:
  0.0 52.4 jit_solution(7982997128042682452)
XLA Ops:
  0.0 1.0 %fusion.239 = (f32[3,2,16,4]{3,2,1,0:T(8,128)S(1)}, f32[3,2,16,4]{3,2,1,0:T(8,128)S(1)}) fusion(f32[3,2,16,128]{3,2,1,0:T(8,128)} %param.5), kind=kLoop, calls=%fused_computation.385 | loop fusion | bytes 6144 | tf_op jit(solution)/shard_map/slice | solution.py:19
  1.0 3.0 %collective-permute-start = (f32[3,2,16,4]{3,2,1,0:T(8,128)S(1)}, f32[3,2,16,4]{3,2,1,0:T(8,128)S(1)}, u32[]{:S(2)}, u32[]{:S(2)}) collective-permute-start(f32[3,2,16,4]{3,2,1,0:T(8,128)S(1)} %get-tuple-element.59), channel_id=1, source_target_pairs={{0,1},{1,0},{2,3},{3,2},{4,5},{5,4},{6,7},{7,6},{8,9},{9,8},{10,11... | collective-permute-start | bytes 4616 | tf_op jit(solution)/shard_map/ppermute | solution.py:22
  4.1 0.7 %copy-done.2 = f32[1,1,256]{2,1,0:T(1,128)S(1)} copy-done((f32[1,1,256]{2,1,0:T(1,128)S(1)}, f32[1,1,256]{2,1,0:T(1,128)}, u32[]{:S(2)}) %copy-start.2) | copy-done | bytes 1048
  4.8 1.3 %collective-permute-done = f32[3,2,16,4]{3,2,1,0:T(8,128)S(1)} collective-permute-done((f32[3,2,16,4]{3,2,1,0:T(8,128)S(1)}, f32[3,2,16,4]{3,2,1,0:T(8,128)S(1)}, u32[]{:S(2)}, u32[]{:S(2)}) %collective-permute-start) | collective-permute-done | bytes 1568 | tf_op jit(solution)/shard_map/ppermute | solution.py:22
  6.1 2.0 %collective-permute-done.1 = f32[3,2,16,4]{3,2,1,0:T(8,128)S(1)} collective-permute-done((f32[3,2,16,4]{3,2,1,0:T(8,128)S(1)}, f32[3,2,16,4]{3,2,1,0:T(8,128)S(1)}, u32[]{:S(2)}, u32[]{:S(2)}) %collective-permute-start.1) | collective-permute-done | bytes 1568 | tf_op jit(solution)/shard_map/ppermute | solution.py:24
  8.1 0.1 pad_maximum_fusion
  8.2 0.1 fusion.299
  8.8 0.1 fusion.140
  9.0 0.1 fusion.136
  9.1 0.1 pad_maximum_fusion.1
  9.9 0.1 fusion.121
  10.1 0.1 fusion.117
  10.2 0.1 pad_maximum_fusion.2
  10.9 0.1 fusion.102
  11.1 0.1 fusion.98
  11.2 0.1 slice_add_fusion.3
  12.0 0.1 fusion.208
  12.2 0.1 fusion.33
  12.4 0.7 %copy.57 = f32[3,2,16,128]{3,0,1,2:T(4,128)} copy(f32[3,2,16,128]{3,2,1,0:T(8,128)S(1)} %fusion.33) | data formatting | bytes 98304 | tf_op jit(solution)/shard_map/add | solution.py:71
  13.0 5.9 %all-to-all-start = ((f32[3,2,16,128]{3,0,1,2:T(4,128)}), f32[3,2,16,128]{3,0,1,2:T(4,128)S(1)}, u32[]{:S(2)}, u32[]{:S(2)}) async-start(f32[3,2,16,128]{3,0,1,2:T(4,128)} %copy.57), calls=%async_computation | async-start | bytes 131072 | tf_op jit(solution)/shard_map/all_to_all | solution.py:119
  19.0 6.9 %all-to-all-done = f32[3,2,16,128]{3,0,1,2:T(4,128)S(1)} async-done(((f32[3,2,16,128]{3,0,1,2:T(4,128)}), f32[3,2,16,128]{3,0,1,2:T(4,128)S(1)}, u32[]{:S(2)}, u32[]{:S(2)}) %all-to-all-start) | async-done | bytes 49184 | tf_op jit(solution)/shard_map/all_to_all | solution.py:119
  25.9 0.1 copy.59
  26.0 0.7 %gather_fusion = f32[256,32]{1,0:T(8,128)S(1)} fusion(f32[384,32]{1,0:T(8,128)S(1)} %bitcast.274, s32[1024]{0:T(1024)S(1)} %pad_clamp_fusion), kind=kCustom, calls=%fused_computation | custom fusion | bytes 66560 | tf_op jit(solution)/shard_map/jit(take_along_axis)/gather | solution.py:94
  26.8 0.2 fusion.13
  26.9 1.2 %multiply_reduce_fusion = (f32[]{:T(128)}, f32[32,32]{1,0:T(8,128)S(1)}) fusion(f32[256,32]{1,0:T(8,128)S(1)} %gather_fusion, f32[256]{0:T(256)S(1)} %broadcast_multiply_fusion.1, pred[256]{0:T(512)(128)(4,1)S(1)} %compare_and_fusion, f32[256]{0:T(256)S(1)} %bitcast.283), kind=kOutput, calls=%fused_computation.366 | convolution fusion | flops 3191807 | bytes 39172 | tf_op jit(solution)/shard_map/rboi,rboj->rbij/dot_general | solution.py:98
  28.8 0.1 fusion.7
  28.9 0.1 fusion.233
  29.1 0.1 fusion.230
  29.2 0.2 fusion.6
  29.4 0.1 fusion.305
  29.5 0.1 fusion.304
  29.7 0.2 fusion.5
  29.8 0.1 fusion.307
  30.0 0.1 fusion.306
  30.1 0.2 fusion.4
  30.3 0.1 fusion.309
  30.4 0.1 fusion.308
  30.6 0.2 fusion.3
  30.8 0.1 fusion.311
  30.9 0.1 fusion.310
  31.1 0.2 fusion.2
  31.2 0.1 fusion.312
  31.4 0.2 convolution_divide_fusion
  31.7 0.7 %copy-done.4 = f32[1,1,256]{2,1,0:T(1,128)S(1)} copy-done((f32[1,1,256]{2,1,0:T(1,128)S(1)}, f32[1,1,256]{2,1,0:T(1,128)}, u32[]{:S(2)}) %copy-start.4) | copy-done | bytes 1048
  32.4 0.3 convolution_bitcast_fusion.2
  32.7 0.1 convolution_bitcast_fusion.1
  32.9 0.3 fusion.1
  33.3 9.3 %all_to_all.33 = f32[3,32,1,128]{3,2,0,1:T(1,128)S(1)} all-to-all(f32[3,32,1,128]{3,2,0,1:T(1,128)S(1)} %copy.62), channel_id=1, replica_groups=mesh['mem'=16,'tile'=2] {'mem'}, dimensions={1} | all-to-all | bytes 98304 | tf_op jit(solution)/shard_map/all_to_all | solution.py:125
  42.7 0.5 %collective-permute-start.2 = (f32[3,2,16,4]{3,2,1,0:T(8,128)S(1)}, f32[3,2,16,4]{3,2,1,0:T(8,128)S(1)}, u32[]{:S(2)}, u32[]{:S(2)}) collective-permute-start(f32[3,2,16,4]{3,2,1,0:T(8,128)S(1)} %get-tuple-element.57), channel_id=1, source_target_pairs={{0,1},{1,0},{2,3},{3,2},{4,5},{5,4},{6,7},{7,6},{8,9},{9,8},{10,11... | collective-permute-start | bytes 4616 | tf_op jit(solution)/shard_map/ppermute | solution.py:22
  43.3 1.5 %collective-permute-start.3 = (f32[3,2,16,4]{3,2,1,0:T(8,128)S(1)}, f32[3,2,16,4]{3,2,1,0:T(8,128)S(1)}, u32[]{:S(2)}, u32[]{:S(2)}) collective-permute-start(f32[3,2,16,4]{3,2,1,0:T(8,128)S(1)} %get-tuple-element.58), channel_id=1, source_target_pairs={{1,0},{0,1},{3,2},{2,3},{5,4},{4,5},{7,6},{6,7},{9,8},{8,9},{11,10... | collective-permute-start | bytes 4616 | tf_op jit(solution)/shard_map/ppermute | solution.py:24
  44.7 2.1 %collective-permute-done.2 = f32[3,2,16,4]{3,2,1,0:T(8,128)S(1)} collective-permute-done((f32[3,2,16,4]{3,2,1,0:T(8,128)S(1)}, f32[3,2,16,4]{3,2,1,0:T(8,128)S(1)}, u32[]{:S(2)}, u32[]{:S(2)}) %collective-permute-start.2) | collective-permute-done | bytes 1568 | tf_op jit(solution)/shard_map/ppermute | solution.py:22
  46.8 0.5 %collective-permute-done.3 = f32[3,2,16,4]{3,2,1,0:T(8,128)S(1)} collective-permute-done((f32[3,2,16,4]{3,2,1,0:T(8,128)S(1)}, f32[3,2,16,4]{3,2,1,0:T(8,128)S(1)}, u32[]{:S(2)}, u32[]{:S(2)}) %collective-permute-start.3) | collective-permute-done | bytes 1568 | tf_op jit(solution)/shard_map/ppermute | solution.py:24
  47.3 0.1 pad_maximum_fusion.4
  48.1 0.1 fusion.83
  48.3 0.1 fusion.79
  48.4 0.1 pad_maximum_fusion.5
  49.2 0.1 fusion.64
  49.4 0.1 fusion.60
  49.5 0.1 pad_maximum_fusion.6
  50.3 0.1 fusion.45
  50.5 0.1 fusion.41
  50.6 0.1 slice_add_fusion
  51.3 0.1 fusion.189
  51.6 0.7 %fusion.28 = f32[3,2,16,128]{3,2,1,0:T(8,128)} fusion(f32[3,2,16,130]{3,2,1,0:T(8,128)S(1)} %get-tuple-element.11, f32[3,2,16,132]{3,2,1,0:T(8,128)S(1)} %get-tuple-element.14, f32[3,2,16,134]{3,2,1,0:T(8,128)S(1)} %get-tuple-element.12, f32[1,2,16,128]{3,2,1,0:T(8,128)S(1)} %fusion.185, f32[1,2,16,128]{3,2,1,0:T(8,128)S(1)} %fusion.189, ...), kind=kLoop, calls=%fused_computation.55 | loop fusion | flops 110592 | bytes 294912 | tf_op jit(solution)/shard_map/add | solution.py:71
  (110 shorter events, 6.2 us)
Async XLA Ops:
  0.0 8.1 %copy-start = (f32[3,2,16,128]{3,2,1,0:T(8,128)S(1)}, f32[3,2,16,128]{3,2,1,0:T(8,128)}, u32[]{:S(2)}) copy-start(f32[3,2,16,128]{3,2,1,0:T(8,128)} %param.5) | copy-start | bytes 147460
  1.0 3.1 %copy-start.3 = (s32[1,1,256]{2,1,0:T(1,128)S(1)}, s32[1,1,256]{2,1,0:T(1,128)}, u32[]{:S(2)}) copy-start(s32[1,1,256]{2,1,0:T(1,128)} %param.6) | copy-start | bytes 3076
  1.0 5.1 %collective-permute-start = (f32[3,2,16,4]{3,2,1,0:T(8,128)S(1)}, f32[3,2,16,4]{3,2,1,0:T(8,128)S(1)}, u32[]{:S(2)}, u32[]{:S(2)}) collective-permute-start(f32[3,2,16,4]{3,2,1,0:T(8,128)S(1)} %get-tuple-element.59), channel_id=1, source_target_pairs={{0,1},{1,0},{2,3},{3,2},{4,5},{5,4},{6,7},{7,6},{8,9},{9,8},{10,11... | collective-permute-start | bytes 4616 | tf_op jit(solution)/shard_map/ppermute | solution.py:22
  4.0 4.1 %collective-permute-start.1 = (f32[3,2,16,4]{3,2,1,0:T(8,128)S(1)}, f32[3,2,16,4]{3,2,1,0:T(8,128)S(1)}, u32[]{:S(2)}, u32[]{:S(2)}) collective-permute-start(f32[3,2,16,4]{3,2,1,0:T(8,128)S(1)} %get-tuple-element.60), channel_id=1, source_target_pairs={{1,0},{0,1},{3,2},{2,3},{5,4},{4,5},{7,6},{6,7},{9,8},{8,9},{11,10... | collective-permute-start | bytes 4616 | tf_op jit(solution)/shard_map/ppermute | solution.py:24
  4.1 0.7 %copy-start.2 = (f32[1,1,256]{2,1,0:T(1,128)S(1)}, f32[1,1,256]{2,1,0:T(1,128)}, u32[]{:S(2)}) copy-start(f32[1,1,256]{2,1,0:T(1,128)} %param.8) | copy-start | bytes 3076
  4.1 0.7 %copy-start.1 = (f32[1,1,256]{2,1,0:T(1,128)S(1)}, f32[1,1,256]{2,1,0:T(1,128)}, u32[]{:S(2)}) copy-start(f32[1,1,256]{2,1,0:T(1,128)} %param.9) | copy-start | bytes 3076
  13.0 12.8 %all-to-all-start = ((f32[3,2,16,128]{3,0,1,2:T(4,128)}), f32[3,2,16,128]{3,0,1,2:T(4,128)S(1)}, u32[]{:S(2)}, u32[]{:S(2)}) async-start(f32[3,2,16,128]{3,0,1,2:T(4,128)} %copy.57), calls=%async_computation | async-start | bytes 131072 | tf_op jit(solution)/shard_map/all_to_all | solution.py:119
  31.7 0.7 %copy-start.4 = (f32[1,1,256]{2,1,0:T(1,128)S(1)}, f32[1,1,256]{2,1,0:T(1,128)}, u32[]{:S(2)}) copy-start(f32[1,1,256]{2,1,0:T(1,128)} %param.7) | copy-start | bytes 3076
  42.7 4.1 %collective-permute-start.2 = (f32[3,2,16,4]{3,2,1,0:T(8,128)S(1)}, f32[3,2,16,4]{3,2,1,0:T(8,128)S(1)}, u32[]{:S(2)}, u32[]{:S(2)}) collective-permute-start(f32[3,2,16,4]{3,2,1,0:T(8,128)S(1)} %get-tuple-element.57), channel_id=1, source_target_pairs={{0,1},{1,0},{2,3},{3,2},{4,5},{5,4},{6,7},{7,6},{8,9},{9,8},{10,11... | collective-permute-start | bytes 4616 | tf_op jit(solution)/shard_map/ppermute | solution.py:22
  43.3 4.1 %collective-permute-start.3 = (f32[3,2,16,4]{3,2,1,0:T(8,128)S(1)}, f32[3,2,16,4]{3,2,1,0:T(8,128)S(1)}, u32[]{:S(2)}, u32[]{:S(2)}) collective-permute-start(f32[3,2,16,4]{3,2,1,0:T(8,128)S(1)} %get-tuple-element.58), channel_id=1, source_target_pairs={{1,0},{0,1},{3,2},{2,3},{5,4},{4,5},{7,6},{6,7},{9,8},{8,9},{11,10... | collective-permute-start | bytes 4616 | tf_op jit(solution)/shard_map/ppermute | solution.py:24
where the time goes:
time: 52.7 us; the launch traced here: 52.4 us
  waiting for transfers between devices  12.8 us (24%)
  starting transfers between devices  11.1 us (21%)
  blocking collectives  9.34 us (18%)
  local copies, waits for them, and re-layouts  9.04 us (17%)
  matrix products  4.63 us (9%)
  other arithmetic  4.22 us (8%)
  between operations  1.26 us (2%)
    all_to_all x1, blocking collectives, local(): lax.all_to_all(updated_member_set.reshape(3, members, row_count, columns)...  9.34 us
    all_to_all x1, waiting for transfers between devices, local(): lax.all_to_all(background_member_set, 'mem', split_axis=2, concat_axis=1,...  6.88 us
    all_to_all x1, starting transfers between devices, local(): lax.all_to_all(background_member_set, 'mem', split_axis=2, concat_axis=1,...  5.94 us
    slice x62, local copies, waits for them, and re-layouts, along(): return (jnp.roll(inner, -1, -2) - jnp.roll(inner, 1, -2)) * 0.5  4.91 us
    ppermute x2, starting transfers between devices, with_halo(): lax.ppermute(tail, axis, [(i, (i + 1) % count) for i in range(count)])  3.57 us
    ppermute x2, waiting for transfers between devices, with_halo(): lax.ppermute(tail, axis, [(i, (i + 1) % count) for i in range(count)])  3.35 us
    dot_general x18, matrix products, product(): return jnp.einsum('rbij,rbjk->rbik', left, right, precision=highest)  2.66 us
    another operation x28, other arithmetic, tendency(): return jnp.stack([d_height, d_east, d_north])  2.64 us
  transfers between devices with their start and end apart: 5, of which 5 were waited for; matrix products, arithmetic and copies ran while one was open for 0% of the time, Pallas kernels for 0%

commit v1 on v0

--- a/solution.py
+++ b/solution.py
@@ -122,12 +122,20 @@
     columns = patches.shape[3]
     blocks = patches.reshape(3, members, row_count, columns // PCELL, PCELL)
     updated_member_set = analyse(blocks, obs_index, obs_value, obs_var, loc_weight)
-    closing_solution = lax.all_to_all(
-        updated_member_set.reshape(3, members, row_count, columns),
-        "mem",
-        split_axis=1,
-        concat_axis=2,
-        tiled=True,
+    closing_solution = jnp.concatenate(
+        lax.all_to_all(
+            jnp.stack(
+                jnp.split(
+                    updated_member_set.reshape(3, members, row_count, columns),
+                    lax.axis_size("mem"),
+                    axis=1,
+                )
+            ),
+            "mem",
+            0,
+            0,
+        ),
+        axis=2,
     )
     return lead_interval_number(closing_solution)
 

time: 52.7 us -> 52.7 us (level)
    unnamed x10 -> x25, local copies, waits for them, and re-layouts: 1.35 us -> 1.51 us
where the time goes in v1:
time: 52.7 us; the launch traced here: 52.4 us
  waiting for transfers between devices  12.7 us (24%)
  starting transfers between devices  11.1 us (21%)
  blocking collectives  9.34 us (18%)
  local copies, waits for them, and re-layouts  9.13 us (17%)
  matrix products  4.63 us (9%)
  other arithmetic  4.22 us (8%)
  between operations  1.32 us (3%)
    all_to_all x1, blocking collectives, local(): lax.all_to_all(jnp.stack(jnp.split(updated_member_set.reshape(3, members,...  9.34 us
    all_to_all x1, waiting for transfers between devices, local(): lax.all_to_all(background_member_set, 'mem', split_axis=2, concat_axis=1,...  6.75 us
    all_to_all x1, starting transfers between devices, local(): lax.all_to_all(background_member_set, 'mem', split_axis=2, concat_axis=1,...  5.94 us
    slice x62, local copies, waits for them, and re-layouts, along(): return (jnp.roll(inner, -1, -2) - jnp.roll(inner, 1, -2)) * 0.5  4.91 us
    ppermute x2, starting transfers between devices, with_halo(): lax.ppermute(tail, axis, [(i, (i + 1) % count) for i in range(count)])  3.57 us
    ppermute x2, waiting for transfers between devices, with_halo(): lax.ppermute(tail, axis, [(i, (i + 1) % count) for i in range(count)])  3.35 us
    dot_general x18, matrix products, product(): return jnp.einsum('rbij,rbjk->rbik', left, right, precision=highest)  2.66 us
    another operation x28, other arithmetic, tendency(): return jnp.stack([d_height, d_east, d_north])  2.64 us
  transfers between devices with their start and end apart: 5, of which 5 were waited for; matrix products, arithmetic and copies ran while one was open for 0% of the time, Pallas kernels for 0%

profile of v1, /device:TPU:0, one launch (start us, length us, event | category | flops | bytes accessed | tf_op | source)
XLA Modules:
  0.0 52.4 jit_solution(4519805021748958337)
XLA Ops:
  0.0 1.0 %fusion.239 = (f32[3,2,16,4]{3,2,1,0:T(8,128)S(1)}, f32[3,2,16,4]{3,2,1,0:T(8,128)S(1)}) fusion(f32[3,2,16,128]{3,2,1,0:T(8,128)} %param.5), kind=kLoop, calls=%fused_computation.417 | loop fusion | bytes 6144 | tf_op jit(solution)/shard_map/slice | solution.py:19
  1.0 3.0 %collective-permute-start = (f32[3,2,16,4]{3,2,1,0:T(8,128)S(1)}, f32[3,2,16,4]{3,2,1,0:T(8,128)S(1)}, u32[]{:S(2)}, u32[]{:S(2)}) collective-permute-start(f32[3,2,16,4]{3,2,1,0:T(8,128)S(1)} %get-tuple-element.59), channel_id=1, source_target_pairs={{0,1},{1,0},{2,3},{3,2},{4,5},{5,4},{6,7},{7,6},{8,9},{9,8},{10,11... | collective-permute-start | bytes 4616 | tf_op jit(solution)/shard_map/ppermute | solution.py:22
  4.1 0.7 %copy-done.2 = f32[1,1,256]{2,1,0:T(1,128)S(1)} copy-done((f32[1,1,256]{2,1,0:T(1,128)S(1)}, f32[1,1,256]{2,1,0:T(1,128)}, u32[]{:S(2)}) %copy-start.2) | copy-done | bytes 1048
  4.8 1.3 %collective-permute-done = f32[3,2,16,4]{3,2,1,0:T(8,128)S(1)} collective-permute-done((f32[3,2,16,4]{3,2,1,0:T(8,128)S(1)}, f32[3,2,16,4]{3,2,1,0:T(8,128)S(1)}, u32[]{:S(2)}, u32[]{:S(2)}) %collective-permute-start) | collective-permute-done | bytes 1568 | tf_op jit(solution)/shard_map/ppermute | solution.py:22
  6.1 2.0 %collective-permute-done.1 = f32[3,2,16,4]{3,2,1,0:T(8,128)S(1)} collective-permute-done((f32[3,2,16,4]{3,2,1,0:T(8,128)S(1)}, f32[3,2,16,4]{3,2,1,0:T(8,128)S(1)}, u32[]{:S(2)}, u32[]{:S(2)}) %collective-permute-start.1) | collective-permute-done | bytes 1568 | tf_op jit(solution)/shard_map/ppermute | solution.py:24
  8.1 0.1 pad_maximum_fusion
  8.2 0.1 fusion.299
  8.8 0.1 fusion.140
  9.0 0.1 fusion.136
  9.1 0.1 pad_maximum_fusion.1
  9.9 0.1 fusion.121
  10.1 0.1 fusion.117
  10.2 0.1 pad_maximum_fusion.2
  10.9 0.1 fusion.102
  11.1 0.1 fusion.98
  11.2 0.1 slice_add_fusion.3
  12.0 0.1 fusion.208
  12.2 0.1 fusion.33
  12.4 0.6 %copy.54 = f32[3,2,16,128]{3,1,0,2:T(2,128)} copy(f32[3,2,16,128]{3,2,1,0:T(8,128)S(1)} %fusion.33) | data formatting | bytes 98304 | tf_op jit(solution)/shard_map/add | solution.py:71
  13.0 5.9 %all-to-all-start = ((f32[3,2,16,128]{3,1,0,2:T(2,128)}), f32[3,2,16,128]{3,1,0,2:T(2,128)S(1)}, u32[]{:S(2)}, u32[]{:S(2)}) async-start(f32[3,2,16,128]{3,1,0,2:T(2,128)} %copy.54), calls=%async_computation | async-start | bytes 98304 | tf_op jit(solution)/shard_map/all_to_all | solution.py:119
  19.0 6.8 %all-to-all-done = f32[3,2,16,128]{3,1,0,2:T(2,128)S(1)} async-done(((f32[3,2,16,128]{3,1,0,2:T(2,128)}), f32[3,2,16,128]{3,1,0,2:T(2,128)S(1)}, u32[]{:S(2)}, u32[]{:S(2)}) %all-to-all-start) | async-done | bytes 49184 | tf_op jit(solution)/shard_map/all_to_all | solution.py:119
  25.7 0.1 copy.56
  25.9 0.7 %gather_fusion = f32[256,32]{1,0:T(8,128)S(1)} fusion(f32[384,32]{1,0:T(8,128)S(1)} %bitcast.337, s32[1024]{0:T(1024)S(1)} %pad_clamp_fusion), kind=kCustom, calls=%fused_computation | custom fusion | bytes 66560 | tf_op jit(solution)/shard_map/jit(take_along_axis)/gather | solution.py:94
  26.6 0.2 fusion.13
  26.8 1.2 %multiply_reduce_fusion = (f32[]{:T(128)}, f32[32,32]{1,0:T(8,128)S(1)}) fusion(f32[256,32]{1,0:T(8,128)S(1)} %gather_fusion, f32[256]{0:T(256)S(1)} %broadcast_multiply_fusion.1, pred[256]{0:T(512)(128)(4,1)S(1)} %compare_and_fusion, f32[256]{0:T(256)S(1)} %bitcast.344), kind=kOutput, calls=%fused_computation.382 | convolution fusion | flops 3191807 | bytes 39172 | tf_op jit(solution)/shard_map/rboi,rboj->rbij/dot_general | solution.py:98
  28.7 0.1 fusion.7
  28.8 0.1 fusion.233
  28.9 0.1 fusion.230
  29.1 0.2 fusion.6
  29.2 0.1 fusion.305
  29.4 0.1 fusion.304
  29.5 0.2 fusion.5
  29.7 0.1 fusion.307
  29.8 0.1 fusion.306
  30.0 0.2 fusion.4
  30.2 0.1 fusion.309
  30.3 0.1 fusion.308
  30.4 0.2 fusion.3
  30.6 0.1 fusion.311
  30.8 0.1 fusion.310
  30.9 0.2 fusion.2
  31.1 0.1 fusion.312
  31.2 0.2 convolution_divide_fusion
  31.6 0.7 %copy-done.4 = f32[1,1,256]{2,1,0:T(1,128)S(1)} copy-done((f32[1,1,256]{2,1,0:T(1,128)S(1)}, f32[1,1,256]{2,1,0:T(1,128)}, u32[]{:S(2)}) %copy-start.4) | copy-done | bytes 1048
  32.3 0.3 convolution_bitcast_fusion.2
  32.6 0.1 convolution_bitcast_fusion.1
  32.7 0.3 fusion.1
  33.3 9.3 %all_to_all.20 = f32[16,3,2,1,128]{4,2,1,3,0:T(2,128)S(1)} all-to-all(f32[16,3,2,1,128]{4,2,1,3,0:T(2,128)S(1)} %constant_dynamic-update-slice_fusion), channel_id=1, replica_groups=mesh['mem'=16,'tile'=2] {'mem'}, dimensions={0} | all-to-all | bytes 98304 | tf_op jit(solution)/shard_map/all_to_all | solution.py:126
  42.7 0.5 %collective-permute-start.2 = (f32[3,2,16,4]{3,2,1,0:T(8,128)S(1)}, f32[3,2,16,4]{3,2,1,0:T(8,128)S(1)}, u32[]{:S(2)}, u32[]{:S(2)}) collective-permute-start(f32[3,2,16,4]{3,2,1,0:T(8,128)S(1)} %get-tuple-element.57), channel_id=1, source_target_pairs={{0,1},{1,0},{2,3},{3,2},{4,5},{5,4},{6,7},{7,6},{8,9},{9,8},{10,11... | collective-permute-start | bytes 4616 | tf_op jit(solution)/shard_map/ppermute | solution.py:22
  43.3 1.5 %collective-permute-start.3 = (f32[3,2,16,4]{3,2,1,0:T(8,128)S(1)}, f32[3,2,16,4]{3,2,1,0:T(8,128)S(1)}, u32[]{:S(2)}, u32[]{:S(2)}) collective-permute-start(f32[3,2,16,4]{3,2,1,0:T(8,128)S(1)} %get-tuple-element.58), channel_id=1, source_target_pairs={{1,0},{0,1},{3,2},{2,3},{5,4},{4,5},{7,6},{6,7},{9,8},{8,9},{11,10... | collective-permute-start | bytes 4616 | tf_op jit(solution)/shard_map/ppermute | solution.py:24
  44.8 2.1 %collective-permute-done.2 = f32[3,2,16,4]{3,2,1,0:T(8,128)S(1)} collective-permute-done((f32[3,2,16,4]{3,2,1,0:T(8,128)S(1)}, f32[3,2,16,4]{3,2,1,0:T(8,128)S(1)}, u32[]{:S(2)}, u32[]{:S(2)}) %collective-permute-start.2) | collective-permute-done | bytes 1568 | tf_op jit(solution)/shard_map/ppermute | solution.py:22
  46.8 0.5 %collective-permute-done.3 = f32[3,2,16,4]{3,2,1,0:T(8,128)S(1)} collective-permute-done((f32[3,2,16,4]{3,2,1,0:T(8,128)S(1)}, f32[3,2,16,4]{3,2,1,0:T(8,128)S(1)}, u32[]{:S(2)}, u32[]{:S(2)}) %collective-permute-start.3) | collective-permute-done | bytes 1568 | tf_op jit(solution)/shard_map/ppermute | solution.py:24
  47.4 0.1 pad_maximum_fusion.4
  48.2 0.1 fusion.83
  48.4 0.1 fusion.79
  48.5 0.1 pad_maximum_fusion.5
  49.2 0.1 fusion.64
  49.4 0.1 fusion.60
  49.5 0.1 pad_maximum_fusion.6
  50.3 0.1 fusion.45
  50.5 0.1 fusion.41
  50.6 0.1 slice_add_fusion
  51.4 0.1 fusion.189
  51.6 0.7 %fusion.28 = f32[3,2,16,128]{3,2,1,0:T(8,128)} fusion(f32[3,2,16,130]{3,2,1,0:T(8,128)S(1)} %get-tuple-element.11, f32[3,2,16,132]{3,2,1,0:T(8,128)S(1)} %get-tuple-element.14, f32[3,2,16,134]{3,2,1,0:T(8,128)S(1)} %get-tuple-element.12, f32[1,2,16,128]{3,2,1,0:T(8,128)S(1)} %fusion.185, f32[1,2,16,128]{3,2,1,0:T(8,128)S(1)} %fusion.189, ...), kind=kLoop, calls=%fused_computation.55 | loop fusion | flops 110592 | bytes 294912 | tf_op jit(solution)/shard_map/add | solution.py:71
  (124 shorter events, 6.3 us)
Async XLA Ops:
  0.0 8.1 %copy-start = (f32[3,2,16,128]{3,2,1,0:T(8,128)S(1)}, f32[3,2,16,128]{3,2,1,0:T(8,128)}, u32[]{:S(2)}) copy-start(f32[3,2,16,128]{3,2,1,0:T(8,128)} %param.5) | copy-start | bytes 147460
  1.0 3.1 %copy-start.3 = (s32[1,1,256]{2,1,0:T(1,128)S(1)}, s32[1,1,256]{2,1,0:T(1,128)}, u32[]{:S(2)}) copy-start(s32[1,1,256]{2,1,0:T(1,128)} %param.6) | copy-start | bytes 3076
  1.0 5.1 %collective-permute-start = (f32[3,2,16,4]{3,2,1,0:T(8,128)S(1)}, f32[3,2,16,4]{3,2,1,0:T(8,128)S(1)}, u32[]{:S(2)}, u32[]{:S(2)}) collective-permute-start(f32[3,2,16,4]{3,2,1,0:T(8,128)S(1)} %get-tuple-element.59), channel_id=1, source_target_pairs={{0,1},{1,0},{2,3},{3,2},{4,5},{5,4},{6,7},{7,6},{8,9},{9,8},{10,11... | collective-permute-start | bytes 4616 | tf_op jit(solution)/shard_map/ppermute | solution.py:22
  4.0 4.1 %collective-permute-start.1 = (f32[3,2,16,4]{3,2,1,0:T(8,128)S(1)}, f32[3,2,16,4]{3,2,1,0:T(8,128)S(1)}, u32[]{:S(2)}, u32[]{:S(2)}) collective-permute-start(f32[3,2,16,4]{3,2,1,0:T(8,128)S(1)} %get-tuple-element.60), channel_id=1, source_target_pairs={{1,0},{0,1},{3,2},{2,3},{5,4},{4,5},{7,6},{6,7},{9,8},{8,9},{11,10... | collective-permute-start | bytes 4616 | tf_op jit(solution)/shard_map/ppermute | solution.py:24
  4.1 0.7 %copy-start.2 = (f32[1,1,256]{2,1,0:T(1,128)S(1)}, f32[1,1,256]{2,1,0:T(1,128)}, u32[]{:S(2)}) copy-start(f32[1,1,256]{2,1,0:T(1,128)} %param.8) | copy-start | bytes 3076
  4.1 0.7 %copy-start.1 = (f32[1,1,256]{2,1,0:T(1,128)S(1)}, f32[1,1,256]{2,1,0:T(1,128)}, u32[]{:S(2)}) copy-start(f32[1,1,256]{2,1,0:T(1,128)} %param.9) | copy-start | bytes 3076
  13.0 12.7 %all-to-all-start = ((f32[3,2,16,128]{3,1,0,2:T(2,128)}), f32[3,2,16,128]{3,1,0,2:T(2,128)S(1)}, u32[]{:S(2)}, u32[]{:S(2)}) async-start(f32[3,2,16,128]{3,1,0,2:T(2,128)} %copy.54), calls=%async_computation | async-start | bytes 98304 | tf_op jit(solution)/shard_map/all_to_all | solution.py:119
  31.6 0.7 %copy-start.4 = (f32[1,1,256]{2,1,0:T(1,128)S(1)}, f32[1,1,256]{2,1,0:T(1,128)}, u32[]{:S(2)}) copy-start(f32[1,1,256]{2,1,0:T(1,128)} %param.7) | copy-start | bytes 3076
  42.7 4.1 %collective-permute-start.2 = (f32[3,2,16,4]{3,2,1,0:T(8,128)S(1)}, f32[3,2,16,4]{3,2,1,0:T(8,128)S(1)}, u32[]{:S(2)}, u32[]{:S(2)}) collective-permute-start(f32[3,2,16,4]{3,2,1,0:T(8,128)S(1)} %get-tuple-element.57), channel_id=1, source_target_pairs={{0,1},{1,0},{2,3},{3,2},{4,5},{5,4},{6,7},{7,6},{8,9},{9,8},{10,11... | collective-permute-start | bytes 4616 | tf_op jit(solution)/shard_map/ppermute | solution.py:22
  43.3 4.1 %collective-permute-start.3 = (f32[3,2,16,4]{3,2,1,0:T(8,128)S(1)}, f32[3,2,16,4]{3,2,1,0:T(8,128)S(1)}, u32[]{:S(2)}, u32[]{:S(2)}) collective-permute-start(f32[3,2,16,4]{3,2,1,0:T(8,128)S(1)} %get-tuple-element.58), channel_id=1, source_target_pairs={{1,0},{0,1},{3,2},{2,3},{5,4},{4,5},{7,6},{6,7},{9,8},{8,9},{11,10... | collective-permute-start | bytes 4616 | tf_op jit(solution)/shard_map/ppermute | solution.py:24
